TPU v7x, 512 devices: a whole 4x4x16 slice. The times are simulated.
512 devices in a mesh: stn: 64 (over x, y, z_hi, core), chan: 8 (over z_lo).
Axes of the slice: x: 4, y: 4, z: 16 (z_hi: 2, z_lo: 8; z = z_hi * 8 + z_lo), core: 2. Of those that a mesh axis runs over, the one named last changes fastest.
Arguments:
- voltages: bfloat16 [512, 2, 2, 8, 4864], P('stn', None, None, 'chan'), may hold values from -6 to 6
- prototype: float32 [16, 256], replicated, may hold values from -1.5 to 1.5
- kernel_table: float32 [8, 7], replicated, may hold values from 0.05 to 1
- tile_subgrid: int32 [8, 512, 4, 512, 1], P('chan', 'stn'), may hold values from 0 to 31; in each aligned block of 16384 rows (0 to 16383, 16384 to 32767, ..., all dimensions but the last counted through in order) at most 1024 rows name the same one
- tile_cells: int32 [8, 512, 4, 512, 2], P('chan', 'stn'), may hold values from 3 to 44
- tile_offsets: int32 [8, 512, 4, 512, 2], P('chan', 'stn'), may hold values from 0 to 7
- subgrid_slot: int32 [32], replicated, may hold values from 0 to 31, each once
Outputs:
- uv_grid: float32 [32, 48, 384], P('chan', None, 'stn')
Inputs may be any that keep to these rules, and one draw needn't show every extreme that they name: `tile_subgrid`: among the tiles of one device (one coarse channel c and the 8 stations a of one index of stn), no subgrid is named more than 1024 times, and in every draw some device's tiles name some subgrid exactly 1024 times. `subgrid_slot`: each of 0 to 31 appears once.
All inputs are finite; a program needn't handle non-finite values.
Results may differ from a plain program's by a relative error of at most 0.0066.
Values may be sent and summed in bfloat16 or wider, within the bound.
No kernel may reach another device: no remote copies, remote signals or barrier semaphores. Data moves between devices by JAX's collectives and lax.ppermute only.
A program may use at most 128 MiB of HBM per device.

v0:
```python
import math
import jax
import jax.numpy as jnp
from jax import lax
from jax.sharding import PartitionSpec as P

FINE = 256
TAPS = 16
FRAMES = 4
CT = 4
G = 48
NSUB = 32
KW = 7


def fourier_table(length):
    index = jnp.arange(length, dtype=jnp.int32)
    phase = index[:, None] * index[None, :] % length
    angle = phase.astype(jnp.float32) * (2.0 * math.pi / length)
    cosine = jnp.cos(angle) / math.sqrt(length)
    sine = jnp.sin(angle) / math.sqrt(length)
    upper = jnp.concatenate([cosine, -sine], axis=1)
    lower = jnp.concatenate([sine, cosine], axis=1)
    return jnp.concatenate([upper, lower], axis=0)


def channelize(voltages, prototype):
    stations = voltages.shape[0]
    samples = (
        voltages[:, :, :, 0, :].astype(jnp.float32).reshape(stations, 2, 2, FRAMES + TAPS - 1, FINE)
    )
    filtered = jnp.zeros((stations, 2, 2, FRAMES, FINE), jnp.float32)
    for tap in range(TAPS):
        filtered = filtered + prototype[tap] * samples[:, :, :, tap : tap + FRAMES, :]
    frame_rows = filtered.transpose(0, 1, 3, 2, 4).reshape(stations * 2 * FRAMES, 2 * FINE)
    spectra = jnp.dot(frame_rows, fourier_table(FINE), precision=lax.Precision.HIGHEST).astype(
        jnp.bfloat16
    )
    spectra = spectra.reshape(stations, 2, FRAMES, 2, CT, FINE // CT)
    return spectra.transpose(4, 0, 1, 3, 2, 5).reshape(CT, 2 * stations, 2 * FRAMES * (FINE // CT))


def correlate(mine, theirs):
    tile_count, signal_count, lanes = theirs.shape
    halfway = lanes // 2
    flipped = jnp.concatenate([-theirs[:, :, halfway:], theirs[:, :, :halfway]], axis=2)
    partner = jnp.stack([theirs, flipped], axis=1)
    product = jnp.einsum("tak,tpbk->tapb", mine, partner, preferred_element_type=jnp.float32)
    local_stations = mine.shape[1] // 2
    block_count = signal_count // mine.shape[1]
    product = product.reshape(tile_count, local_stations, 2, 2, block_count, local_stations, 2)
    product = product.transpose(1, 0, 4, 5, 3, 2, 6).reshape(
        local_stations, tile_count, block_count, local_stations, 8
    )
    return (product * (1.0 / halfway)).astype(jnp.bfloat16)


def drop_autos(tiles_all, block_index):
    local_stations, tile_count, block_count, other_stations, comps = tiles_all.shape
    same_block = jnp.arange(block_count, dtype=jnp.int32) == block_index
    same_station = (
        jnp.arange(local_stations, dtype=jnp.int32)[:, None]
        == jnp.arange(other_stations, dtype=jnp.int32)[None, :]
    )
    matched = same_station[:, None, None, :, None] & same_block[None, None, :, None, None]
    return jnp.where(matched, jnp.zeros_like(tiles_all), tiles_all)


def lookup_taps(index, kernel_table):
    choose = (index[:, None] == jnp.arange(kernel_table.shape[0], dtype=jnp.int32)[None, :]).astype(
        jnp.float32
    )
    return jnp.dot(choose, kernel_table, precision=lax.Precision.HIGHEST).astype(jnp.bfloat16)


def spread_taps(taps, centre, extent):
    cells = jnp.arange(extent, dtype=jnp.int32)[:, None]
    placed = jnp.zeros((extent, taps.shape[1]), jnp.float32)
    for offset in range(KW):
        matched = cells == centre[None, :] + (offset - KW // 2)
        placed = jnp.where(matched, taps[offset][None, :].astype(jnp.float32), placed)
    return placed


def grid_slots(payload, cells):
    slot_count = payload.shape[1]
    values = payload[:8].astype(jnp.float32)
    across = spread_taps(payload[8 : 8 + KW], cells[0], G)
    down = spread_taps(payload[8 + KW : 8 + 2 * KW], cells[1], G).astype(jnp.bfloat16)
    weighted = (
        (values[:, None, :] * across[None, :, :]).astype(jnp.bfloat16).reshape(8 * G, slot_count)
    )
    return lax.dot_general(
        down, weighted, (((1,), (1,)), ((), ())), preferred_element_type=jnp.float32
    )


def grid_in_blocks(payload, cells, block_size):
    pieces = payload.shape[1] // block_size
    payload_blocks = payload.reshape(payload.shape[0], pieces, block_size).transpose(1, 0, 2)
    cell_blocks = cells.reshape(2, pieces, block_size).transpose(1, 0, 2)

    def accumulate(total, pair):
        return (total + grid_slots(pair[0], pair[1]), None)

    total, unused = lax.scan(
        accumulate, jnp.zeros((G, 8 * G), jnp.float32), (payload_blocks, cell_blocks)
    )
    return total


def per_device(
    voltages, prototype, kernel_table, tile_subgrid, tile_cells, tile_offsets, subgrid_slot
):
    spectra = channelize(voltages, prototype)
    rank_here = lax.axis_index("stn")
    result = correlate(spectra, lax.all_gather(spectra, "stn", axis=1, tiled=True))
    visible = drop_autos(result, rank_here)
    values = visible.reshape(-1, 8)
    tile_total = values.shape[0]
    slot_depth = 2 * tile_total // NSUB
    subgrid = tile_subgrid.reshape(-1)
    cells = tile_cells.reshape(-1, 2)
    offsets = tile_offsets.reshape(-1, 2)
    places_index = jnp.arange(NSUB, dtype=jnp.int32)[None, :]
    position = jnp.sum(
        jnp.where(subgrid[:, None] == places_index, subgrid_slot[None, :], 0), axis=1
    )
    member = (position[:, None] == places_index).astype(jnp.int32)
    rank = jnp.sum(member * jnp.cumsum(member, axis=0), axis=1) - 1
    target = position * slot_depth + rank
    across = lookup_taps(offsets[:, 0], kernel_table)
    down = lookup_taps(offsets[:, 1], kernel_table)
    payload = jnp.concatenate([values, across, down], axis=1)
    width_pay = payload.shape[1]
    slot_payload = (
        jnp.zeros((width_pay, NSUB * slot_depth), jnp.bfloat16).at[:, target].set(payload.T)
    )
    slot_cells = jnp.zeros((2, NSUB * slot_depth), jnp.int32).at[:, target].set(cells.T)
    slot_payload = slot_payload.reshape(width_pay, NSUB, slot_depth).transpose(1, 0, 2)
    slot_cells = slot_cells.reshape(2, NSUB, slot_depth).transpose(1, 0, 2)
    groups = lax.axis_size("chan")
    owned_count = NSUB // groups
    payloads = lax.all_to_all(
        slot_payload.reshape(groups, owned_count, width_pay, slot_depth),
        "chan",
        split_axis=0,
        concat_axis=3,
        tiled=True,
    )
    placements = lax.all_to_all(
        slot_cells.reshape(groups, owned_count, 2, slot_depth),
        "chan",
        split_axis=0,
        concat_axis=3,
        tiled=True,
    )

    def one_subgrid(pair):
        return grid_in_blocks(pair[0], pair[1], slot_depth)

    owned = lax.map(one_subgrid, (payloads[0], placements[0]))
    return lax.psum_scatter(owned, "stn", scatter_dimension=2, tiled=True)


def solution(mesh):
    return jax.shard_map(
        per_device,
        mesh=mesh,
        in_specs=(
            P("stn", None, None, "chan", None),
            P(),
            P(),
            P("chan", "stn", None, None, None),
            P("chan", "stn", None, None, None),
            P("chan", "stn", None, None, None),
            P(),
        ),
        out_specs=P("chan", None, "stn"),
        check_vma=False,
    )
```

profile of v0, /device:TPU:32, one launch (start us, length us, event | category | flops | bytes accessed | tf_op | source)
XLA Modules:
  0.0 1447.3 jit_solution(1598610117167969650)
XLA Ops:
  6.5 1.1 sine_multiply_fusion
  7.6 1.0 fusion.81
  8.6 1.2 fusion.86
  9.8 1.0 copy.111
  10.9 0.5 fusion.66
  11.6 0.8 convolution_convert_fusion.2
  12.5 0.8 reshape.633
  13.3 0.5 select_reduce_fusion
  14.5 1.6 broadcast_add_fusion.12
  16.1 2.0 copy.110
  18.1 1.7 fusion.40
  19.9 4.9 copy.123
  24.9 47.4 %scatter_custom_fusion.1 = s32[2,32768]{0,1:T(8,128)} fusion(s32[16384]{0:T(1024)S(1)} %bitcast.210, s32[16384,2]{1,0:T(8,128)} %copy.123, s32[]{:T(128)} %constant.50.clone.1), kind=kCustom, calls=%fused_computation.90 | custom fusion | bytes 262656 | tf_op jit(solution)/shard_map/scatter | solution.py:139
  72.3 9.9 copy.124
  82.2 12.6 all-to-all-start.1
  95.2 0.5 broadcast_in_dim.135
  95.8 0.4 convolution_convert_fusion
  96.2 0.4 convolution_convert_fusion.1
  96.6 36.8 %all-gather.2.cloned.1.call-done = bf16[4,1024,512]{2,1,0:T(8,128)(2,1)} async-done(((bf16[4,16,512]{2,1,0:T(8,128)(2,1)}), bf16[4,1024,512]{2,1,0:T(8,128)(2,1)}) %all-gather.2.cloned.1.call-update) | async-done | bytes 4194320 | tf_op jit(solution)/shard_map/all_gather | solution.py:117
  133.4 2.5 slice_negate_fusion
  136.3 1.8 copy-done.2
  138.1 2.7 fusion.46
  140.8 6.1 copy.115
  146.9 33.5 %copy.116 = bf16[8,4,64,8,2,2,2]{3,2,1,0,6,5,4:T(8,128)(2,1)} copy(bf16[8,4,64,8,2,2,2]{1,6,3,2,4,5,0:T(2,128)(2,1)} %bitcast.175) | data formatting | bytes 524288 | tf_op jit(solution)/shard_map/convert_element_type | solution.py:55
  180.4 10.4 convert_element_type.227
  191.1 3.4 copy.118
  194.5 46.3 %scatter_custom_fusion = bf16[22,32768]{0,1:T(8,128)(2,1)} fusion(s32[16384]{0:T(1024)S(1)} %bitcast.211, bf16[16384,22]{1,0:T(8,128)(2,1)} %copy.118, bf16[]{:T(256)} %constant.57.clone.1), kind=kCustom, calls=%fused_computation.93 | custom fusion | bytes 1442304 | tf_op jit(solution)/shard_map/scatter | solution.py:137
  240.7 7.4 copy.119
  248.2 0.6 reshape.636
  248.7 1.7 copy.120
  250.4 32.0 %all-to-all-start = ((bf16[8,4,22,1024]{3,1,2,0:T(4,128)(2,1)}), bf16[8,4,22,1024]{3,1,2,0:T(4,128)(2,1)S(1)}, u32[]{:S(2)}, u32[]{:S(2)}) async-start(bf16[8,4,22,1024]{3,1,2,0:T(4,128)(2,1)} %copy.120), calls=%async_computation | async-start | bytes 2883584 | tf_op jit(solution)/shard_map/all_to_all | solution.py:144
  282.8 63.8 %all-to-all-done = bf16[8,4,22,1024]{3,1,2,0:T(4,128)(2,1)S(1)} async-done(((bf16[8,4,22,1024]{3,1,2,0:T(4,128)(2,1)}), bf16[8,4,22,1024]{3,1,2,0:T(4,128)(2,1)S(1)}, u32[]{:S(2)}, u32[]{:S(2)}) %all-to-all-start) | async-done | bytes 1441824 | tf_op jit(solution)/shard_map/all_to_all | solution.py:144
  346.6 1.9 copy.129
  348.5 2.1 reshape.689
  350.6 29.1 %while.22 = (s32[]{:T(128)}, f32[4,48,384]{2,1,0:T(8,128)S(1)}, bf16[4,22,8192]{2,1,0:T(8,128)(2,1)S(1)}, s32[4,2,8192]{2,1,0:T(2,128)S(1)}, s32[]{:T(128)}, /*i...) while((s32[]{:T(128)}, f32[4,48,384]{2,1,0:T(8,128)S(1)}, ...), condition=%wide.region_9.10_spmd, body=%wide.region_6.9_spmd.sunk | while | flops 39983120 | bytes 5698380 | solution.py:162
  351.2 6.7 while.23
  352.5 0.4 convolution_add_fusion.2
  355.8 0.4 convolution_add_fusion.2
  358.5 6.7 while.23
  358.9 0.4 convolution_add_fusion.2
  365.8 6.7 while.23
  367.0 0.4 convolution_add_fusion.2
  373.0 6.7 while.23
  373.5 0.4 convolution_add_fusion.2
  379.8 1.2 copy.127
  381.0 1.3 dynamic-slice
  382.9 1056.3 %all-reduce.3.cloned.1.call-done = f32[4,48,384]{1,0,2:T(4,128)} async-done(((f32[4,48,384]{1,0,2:T(4,128)}), f32[4,48,384]{1,0,2:T(4,128)}) %all-reduce.3.cloned.1.call-update) | async-done | bytes 294928
  1439.2 1.3 constant_dynamic-slice_fusion.18
  (321 shorter events, 26.9 us)
Async XLA Ops:
  6.5 89.3 %copy-start = (f32[8,7]{1,0:T(8,128)S(1)}, f32[8,7]{1,0:T(8,128)}, u32[]{:S(2)}) copy-start(f32[8,7]{1,0:T(8,128)} %param.13) | copy-start | bytes 676
  6.5 126.9 %all-gather.2.cloned.1.call-start = ((), (), s32[]{:S(2)}) async-start(), calls=%async_computation.2 | async-start | bytes 4259840 | tf_op jit(solution)/shard_map/all_gather | solution.py:117
  11.4 1.9 copy-start.5
  11.4 1.9 copy-start.6
  18.1 1.7 copy-start.3
  72.3 23.4 %copy-start.4 = (s32[1,8,4,512,2]{3,4,2,1,0:T(2,128)S(1)}, s32[1,8,4,512,2]{3,4,2,1,0:T(2,128)}, u32[]{:S(2)}) copy-start(s32[1,8,4,512,2]{3,4,2,1,0:T(2,128)} %param.16) | copy-start | bytes 393220
  82.2 168.3 %all-to-all-start.1 = ((s32[8,4,2,1024]{3,2,1,0:T(2,128)}), s32[8,4,2,1024]{3,2,1,0:T(2,128)S(1)}, u32[]{:S(2)}, u32[]{:S(2)}) async-start(s32[8,4,2,1024]{3,2,1,0:T(2,128)} %bitcast.44), calls=%async_computation.1 | async-start | bytes 524288 | tf_op jit(solution)/shard_map/all_to_all | solution.py:151
  135.9 2.2 copy-start.2
  250.4 96.2 %all-to-all-start = ((bf16[8,4,22,1024]{3,1,2,0:T(4,128)(2,1)}), bf16[8,4,22,1024]{3,1,2,0:T(4,128)(2,1)S(1)}, u32[]{:S(2)}, u32[]{:S(2)}) async-start(bf16[8,4,22,1024]{3,1,2,0:T(4,128)(2,1)} %copy.120), calls=%async_computation | async-start | bytes 2883584 | tf_op jit(solution)/shard_map/all_to_all | solution.py:144
  282.4 1156.8 %all-reduce.3.cloned.1.call-start = ((), (), s32[]{:S(2)}) async-start(), calls=%async_computation.3 | async-start | bytes 1572864
  379.8 1060.7 %copy-start.1 = (f32[8,7]{1,0:T(8,128)S(1)}, f32[8,7]{1,0:T(8,128)}, u32[]{:S(2)}) copy-start(f32[8,7]{1,0:T(8,128)} %param.13) | copy-start | bytes 676
Sparse Core Ops, SparseCore 0:
  13.4 119.9 all-gather.1
  381.1 1058.0 all-reduce.2
where the time goes:
time: 1450 us
  waiting for transfers between devices  1160 us (80%)
  local copies, waits for them, and re-layouts  191 us (13%)
  starting transfers between devices  44.6 us (3%)
  other arithmetic  21.5 us (1%)
  matrix products  16.5 us (1%)
    unnamed x3, waiting for transfers between devices  1060 us
    all_to_all x1, waiting for transfers between devices, per_device(): lax.all_to_all(slot_payload.reshape(groups, owned_count, width_pay, slot_...  63.8 us
    convert_element_type x3, local copies, waits for them, and re-layouts, correlate(): return (product * (1.0 / halfway)).astype(jnp.bfloat16)  50.1 us
    scatter x1, local copies, waits for them, and re-layouts, per_device(): jnp.zeros((2, NSUB * slot_depth), jnp.int32).at[:, target].set(cells.T)  47.4 us
    scatter x1, local copies, waits for them, and re-layouts, per_device(): jnp.zeros((width_pay, NSUB * slot_depth), jnp.bfloat16).at[:, target]  46.3 us
    all_gather x1, waiting for transfers between devices, per_device(): lax.all_gather(spectra, 'stn', axis=1, tiled=True)  36.8 us
    all_to_all x1, starting transfers between devices, per_device(): lax.all_to_all(slot_payload.reshape(groups, owned_count, width_pay, slot_...  32 us
  transfers between devices with their start and end apart: 4, of which 3 were waited for; matrix products, arithmetic and copies ran while one was open for 13% of the time, Pallas kernels for 0%

commit v1 on v0

--- a/solution.py
+++ b/solution.py
@@ -114,7 +114,12 @@
 ):
     spectra = channelize(voltages, prototype)
     rank_here = lax.axis_index("stn")
-    result = correlate(spectra, lax.all_gather(spectra, "stn", axis=1, tiled=True))
+    result = correlate(
+        spectra,
+        jnp.concatenate(
+            lax.all_to_all(jnp.stack([spectra] * lax.axis_size("stn")), "stn", 0, 0), axis=1
+        ),
+    )
     visible = drop_autos(result, rank_here)
     values = visible.reshape(-1, 8)
     tile_total = values.shape[0]

time: 1450 us -> 1530 us (1.055)
  waiting for transfers between devices: 1160 us -> 1240 us
    all_to_all x0 -> x1, waiting for transfers between devices: none -> 123 us  [per_device(): lax.all_to_all(jnp.stack([spectra] * lax.axis_size('stn')), 'stn', 0, 0)]
    all_gather x1 -> x0, waiting for transfers between devices: 36.8 us -> none  [per_device(): lax.all_gather(spectra, 'stn', axis=1, tiled=True)]
    all_to_all x1, starting transfers between devices: 32 us -> 9.91 us  [per_device(): lax.all_to_all(slot_payload.reshape(groups, owned_count, width_pay, slot_...]
    all_to_all x0 -> x1, starting transfers between devices: none -> 21.2 us  [per_device(): lax.all_to_all(jnp.stack([spectra] * lax.axis_size('stn')), 'stn', 0, 0)]
    unnamed x3 -> x2, waiting for transfers between devices: 1060 us -> 1050 us
  transfers between devices with their start and end apart: 4 -> 4, of which waited for: 3 -> 3; matrix products, arithmetic and copies ran while one was open for 13% -> 12% of each run, Pallas kernels for 0% -> 0%
where the time goes in v1:
time: 1530 us; the launch traced here: 1520 us
  waiting for transfers between devices  1240 us (81%)
  local copies, waits for them, and re-layouts  193 us (13%)
  starting transfers between devices  38 us (2%)
  other arithmetic  19.3 us (1%)
  matrix products  16.5 us (1%)
    unnamed x2, waiting for transfers between devices  1050 us
    all_to_all x1, waiting for transfers between devices, per_device(): lax.all_to_all(jnp.stack([spectra] * lax.axis_size('stn')), 'stn', 0, 0)  123 us
    all_to_all x1, waiting for transfers between devices, per_device(): lax.all_to_all(slot_payload.reshape(groups, owned_count, width_pay, slot_...  63.8 us
    convert_element_type x3, local copies, waits for them, and re-layouts, correlate(): return (product * (1.0 / halfway)).astype(jnp.bfloat16)  50.1 us
    scatter x1, local copies, waits for them, and re-layouts, per_device(): jnp.zeros((2, NSUB * slot_depth), jnp.int32).at[:, target].set(cells.T)  47.4 us
    scatter x1, local copies, waits for them, and re-layouts, per_device(): jnp.zeros((width_pay, NSUB * slot_depth), jnp.bfloat16).at[:, target]  46.5 us
  transfers between devices with their start and end apart: 4, of which 3 were waited for; matrix products, arithmetic and copies ran while one was open for 12% of the time, Pallas kernels for 0%

profile of v1, /device:TPU:32, one launch (start us, length us, event | category | flops | bytes accessed | tf_op | source)
XLA Modules:
  0.0 1524.6 jit_solution(16552860831404931075)
XLA Ops:
  6.5 1.1 sine_multiply_fusion
  7.6 1.0 fusion.81
  8.6 1.1 fusion.86
  9.6 1.0 copy.111
  10.8 0.5 fusion.66
  11.4 0.8 convolution_convert_fusion.2
  12.5 2.5 stack.9
  15.0 21.2 %all-to-all-start = ((bf16[64,4,16,512]{3,2,1,0:T(8,128)(2,1)}), bf16[64,4,16,512]{3,2,1,0:T(8,128)(2,1)}, u32[]{:S(2)}, u32[]{:S(2)}) async-start(bf16[64,4,16,512]{3,2,1,0:T(8,128)(2,1)} %stack.9), calls=%async_computation | async-start | bytes 8388608 | tf_op jit(solution)/shard_map/all_to_all | solution.py:120
  36.5 0.5 broadcast_in_dim.135
  37.0 0.5 select_reduce_fusion
  38.2 1.6 broadcast_add_fusion.12
  39.8 2.0 copy.110
  41.8 4.9 copy.124
  46.8 1.7 fusion.40
  48.6 47.4 %scatter_custom_fusion.1 = s32[2,32768]{0,1:T(8,128)} fusion(s32[16384]{0:T(1024)S(1)} %bitcast.211, s32[16384,2]{1,0:T(8,128)} %copy.124, s32[]{:T(128)} %constant.50.clone.1), kind=kCustom, calls=%fused_computation.90 | custom fusion | bytes 262656 | tf_op jit(solution)/shard_map/scatter | solution.py:144
  96.0 9.9 copy.125
  106.0 0.4 convolution_convert_fusion
  106.4 0.4 convolution_convert_fusion.1
  106.8 123.0 %all-to-all-done = bf16[64,4,16,512]{3,2,1,0:T(8,128)(2,1)} async-done(((bf16[64,4,16,512]{3,2,1,0:T(8,128)(2,1)}), bf16[64,4,16,512]{3,2,1,0:T(8,128)(2,1)}, u32[]{:S(2)}, u32[]{:S(2)}) %all-to-all-start) | async-done | bytes 4194336 | tf_op jit(solution)/shard_map/all_to_all | solution.py:120
  229.8 6.9 all-to-all-start.2
  236.8 2.8 copy.114
  240.2 2.7 fusion.46
  242.9 6.1 copy.116
  249.0 33.5 %copy.117 = bf16[8,4,64,8,2,2,2]{3,2,1,0,6,5,4:T(8,128)(2,1)} copy(bf16[8,4,64,8,2,2,2]{1,6,3,2,4,5,0:T(2,128)(2,1)} %bitcast.175) | data formatting | bytes 524288 | tf_op jit(solution)/shard_map/convert_element_type | solution.py:55
  282.6 10.4 convert_element_type.227
  293.3 3.4 copy.119
  296.6 46.5 %scatter_custom_fusion = bf16[22,32768]{0,1:T(8,128)(2,1)} fusion(s32[16384]{0:T(1024)S(1)} %bitcast.212, bf16[16384,22]{1,0:T(8,128)(2,1)} %copy.119, bf16[]{:T(256)} %constant.57.clone.1), kind=kCustom, calls=%fused_computation.93 | custom fusion | bytes 1442304 | tf_op jit(solution)/shard_map/scatter | solution.py:142
  343.1 7.4 copy.120
  350.5 0.6 reshape.646
  351.1 1.7 copy.121
  352.8 9.9 all-to-all-start.1
  363.1 63.8 %all-to-all-done.1 = bf16[8,4,22,1024]{3,1,2,0:T(4,128)(2,1)S(1)} async-done(((bf16[8,4,22,1024]{3,1,2,0:T(4,128)(2,1)}), bf16[8,4,22,1024]{3,1,2,0:T(4,128)(2,1)S(1)}, u32[]{:S(2)}, u32[]{:S(2)}) %all-to-all-start.1) | async-done | bytes 1441824 | tf_op jit(solution)/shard_map/all_to_all | solution.py:149
  426.9 1.9 copy.130
  428.8 2.1 reshape.699
  431.0 29.1 %while.22 = (s32[]{:T(128)}, f32[4,48,384]{2,1,0:T(8,128)S(1)}, bf16[4,22,8192]{2,1,0:T(8,128)(2,1)S(1)}, s32[4,2,8192]{2,1,0:T(2,128)S(1)}, s32[]{:T(128)}, /*i...) while((s32[]{:T(128)}, f32[4,48,384]{2,1,0:T(8,128)S(1)}, ...), condition=%wide.region_9.10_spmd, body=%wide.region_6.9_spmd.sunk | while | flops 39983120 | bytes 5698380 | solution.py:167
  431.5 6.7 while.23
  432.0 0.4 convolution_add_fusion.2
  433.6 0.4 convolution_add_fusion.2
  438.8 6.7 while.23
  440.1 0.4 convolution_add_fusion.2
  446.1 6.7 while.23
  446.5 0.4 convolution_add_fusion.2
  453.4 6.7 while.23
  454.6 0.4 convolution_add_fusion.2
  460.1 1.2 copy.128
  461.3 1.3 dynamic-slice
  463.2 1053.0 %all-reduce.3.cloned.1.call-done = f32[4,48,384]{1,0,2:T(4,128)} async-done(((f32[4,48,384]{1,0,2:T(4,128)}), f32[4,48,384]{1,0,2:T(4,128)}) %all-reduce.3.cloned.1.call-update) | async-done | bytes 294928
  1516.2 1.3 constant_dynamic-slice_fusion.18
  (320 shorter events, 27.3 us)
Async XLA Ops:
  6.5 99.4 %copy-start = (f32[8,7]{1,0:T(8,128)S(1)}, f32[8,7]{1,0:T(8,128)}, u32[]{:S(2)}) copy-start(f32[8,7]{1,0:T(8,128)} %param.13) | copy-start | bytes 676
  15.0 22.0 %copy-start.4 = (s32[1,8,4,512,1]{3,4,2,1,0:T(1,128)S(1)}, s32[1,8,4,512,1]{3,4,2,1,0:T(1,128)}, u32[]{:S(2)}) copy-start(s32[1,8,4,512,1]{3,4,2,1,0:T(1,128)} %param.14) | copy-start | bytes 196612
  15.0 22.0 %copy-start.5 = (s32[32]{0:T(128)S(1)}, s32[32]{0:T(128)}, u32[]{:S(2)}) copy-start(s32[32]{0:T(128)} %param.17) | copy-start | bytes 388
  15.0 214.9 %all-to-all-start = ((bf16[64,4,16,512]{3,2,1,0:T(8,128)(2,1)}), bf16[64,4,16,512]{3,2,1,0:T(8,128)(2,1)}, u32[]{:S(2)}, u32[]{:S(2)}) async-start(bf16[64,4,16,512]{3,2,1,0:T(8,128)(2,1)} %stack.9), calls=%async_computation | async-start | bytes 8388608 | tf_op jit(solution)/shard_map/all_to_all | solution.py:120
  38.2 3.6 copy-start.2
  96.0 9.9 copy-start.3
  229.8 123.0 %all-to-all-start.2 = ((s32[8,4,2,1024]{3,2,1,0:T(2,128)}), s32[8,4,2,1024]{3,2,1,0:T(2,128)S(1)}, u32[]{:S(2)}, u32[]{:S(2)}) async-start(s32[8,4,2,1024]{3,2,1,0:T(2,128)} %bitcast.45), calls=%async_computation.2 | async-start | bytes 524288 | tf_op jit(solution)/shard_map/all_to_all | solution.py:156
  352.8 74.1 %all-to-all-start.1 = ((bf16[8,4,22,1024]{3,1,2,0:T(4,128)(2,1)}), bf16[8,4,22,1024]{3,1,2,0:T(4,128)(2,1)S(1)}, u32[]{:S(2)}, u32[]{:S(2)}) async-start(bf16[8,4,22,1024]{3,1,2,0:T(4,128)(2,1)} %copy.121), calls=%async_computation.1 | async-start | bytes 2883584 | tf_op jit(solution)/shard_map/all_to_all | solution.py:149
  362.7 1153.4 %all-reduce.3.cloned.1.call-start = ((), (), s32[]{:S(2)}) async-start(), calls=%async_computation.3 | async-start | bytes 1572864
  460.1 1057.4 %copy-start.1 = (f32[8,7]{1,0:T(8,128)S(1)}, f32[8,7]{1,0:T(8,128)}, u32[]{:S(2)}) copy-start(f32[8,7]{1,0:T(8,128)} %param.13) | copy-start | bytes 676
Sparse Core Ops, SparseCore 0:
  461.4 1054.7 all-reduce.2
